TPU v7x, 256 devices: a whole 4x4x8 slice. The times are simulated.
256 devices in a mesh: sub: 64 (over y_lo, z, x), blk: 4 (over y_hi, core).
Axes of the slice: x: 4, y: 4 (y_hi: 2, y_lo: 2; y = y_hi * 2 + y_lo), z: 8, core: 2. Of those that a mesh axis runs over, the one named last changes fastest.
Arguments:
- residual: float32 [32, 131072], P(None, ('sub', 'blk')), may hold values from -6 to 6
- fine_inverse: float32 [64, 2560, 2048], P('sub', None, 'blk'), may hold values from -1 to 1.1
- coarse_inverse: float32 [16384, 4, 4096], P('sub', 'blk'), may hold values from -0.5 to 0.5, as said below
- wanted_rows: int32 [64, 2, 256], P('sub'), may hold values from 0 to 2047
- wanted_count: int32 [64, 2], P('sub'), may hold values from 32 to 256, as said below
- aggregate: int32 [131072], P(('sub', 'blk')), may hold values from 0 to 255
Outputs:
- preconditioned: float32 [32, 131072], P(None, ('sub', 'blk'))
Inputs may be any that keep to these rules, and one draw needn't show every extreme that they name: M of the steps is symmetric: coarse_inverse[i, b, s * 64 + q] equals coarse_inverse[s * 256 + b * 64 + q, b2, s2 * 64 + q2] where i = s2 * 256 + b2 * 64 + q2. `wanted_count`: counts vary from side to side; in every draw some subdomain other than the first and last takes exactly 256 rows from one side.
All inputs are finite; a program needn't handle non-finite values.
Results may differ from a plain program's by a relative error of at most 0.000052.
Values sent between devices are 32-bit elements; how exact they have to be, the bound alone decides.
A program may use at most 64 MiB of HBM per device.

v0:
```python
import jax
import jax.numpy as jnp
from jax import lax
from jax.sharding import PartitionSpec as P


def with_halo(cells, sides, width):
    for axis, dim in sides:
        count = lax.axis_size(axis)
        ends = count - 1
        head = lax.slice_in_dim(cells, 0, width, axis=dim)
        tail = lax.slice_in_dim(cells, cells.shape[dim] - width, cells.shape[dim], axis=dim)
        cells = jnp.concatenate(
            [
                lax.ppermute(tail, axis, [(i, (i + 1) % count) for i in range(ends)]),
                cells,
                lax.ppermute(head, axis, [((i + 1) % count, i) for i in range(ends)]),
            ],
            axis=dim,
        )
    return cells


def mask_slots(picked, wanted_total):
    slot_ids = lax.broadcasted_iota(jnp.int32, (1, picked.shape[1]), 1)
    return jnp.where(slot_ids < wanted_total, picked, jnp.zeros_like(picked))


def on_device(residual, fine_inverse, coarse_inverse, wanted_rows, wanted_count, aggregate):
    own_block = lax.all_gather(residual, "blk", axis=1, tiled=True)
    own_len = own_block.shape[1]
    beside = with_halo(own_block, (("sub", 1),), own_len)
    left_raw = jnp.take(beside[:, :own_len], wanted_rows[0, 0], axis=1)
    right_raw = jnp.take(beside[:, 2 * own_len :], wanted_rows[0, 1], axis=1)
    left_halo = mask_slots(left_raw, wanted_count[0, 0])
    right_halo = mask_slots(right_raw, wanted_count[0, 1])
    extended = jnp.concatenate([left_halo, own_block, right_halo], axis=1)
    fine_part = jnp.dot(
        extended,
        fine_inverse[0],
        precision=lax.Precision.HIGHEST,
        preferred_element_type=jnp.float32,
    )
    coarse_table = coarse_inverse[:, 0, :]
    coarse_len = coarse_table.shape[0]
    levels = lax.broadcasted_iota(jnp.int32, (1, coarse_len), 1)
    onehot = (aggregate[:, None] == levels).astype(jnp.float32)
    partial_value = jnp.dot(
        residual, onehot, precision=lax.Precision.HIGHEST, preferred_element_type=jnp.float32
    )
    coarse_share = lax.psum_scatter(partial_value, "blk", scatter_dimension=1, tiled=True)
    partial_solution = lax.dot_general(
        lax.all_gather(coarse_share, "sub", axis=1, tiled=True),
        coarse_table,
        (((1,), (1,)), ((), ())),
        precision=lax.Precision.HIGHEST,
        preferred_element_type=jnp.float32,
    )
    coarse_solution = lax.psum(partial_solution, "blk")
    lifted = lax.dot_general(
        coarse_solution,
        onehot,
        (((1,), (1,)), ((), ())),
        precision=lax.Precision.HIGHEST,
        preferred_element_type=jnp.float32,
    )
    return fine_part + lifted


def solution(mesh):
    in_specs = (
        P(None, ("sub", "blk")),
        P("sub", None, "blk"),
        P("sub", "blk", None),
        P("sub", None, None),
        P("sub", None),
        P(("sub", "blk")),
    )
    out_specs = P(None, ("sub", "blk"))
    return jax.shard_map(
        on_device, mesh=mesh, in_specs=in_specs, out_specs=out_specs, check_vma=False
    )
```

profile of v0, /device:TPU:1, one launch (start us, length us, event | category | flops | bytes accessed | tf_op | source)
XLA Modules:
  0.0 259.5 jit_solution(2096369147131564380)
XLA Ops:
  6.5 0.0 reduce-scatter.4.cloned.1.call-start
  6.5 10.5 %all_gather.6 = f32[32,2048]{1,0:T(8,128)S(1)} all-gather(f32[32,512]{1,0:T(8,128)} %param.8), channel_id=1, replica_groups=mesh['sub'=64,'blk'=4] {'blk'}, dimensions={1}, use_global_device_ids=true | all-gather | bytes 327680 | tf_op jit(solution)/shard_map/all_gather | solution.py:30
  17.1 1.3 collective-permute-start.1
  18.3 4.0 %collective-permute-start = (f32[32,2048]{1,0:T(8,128)S(1)}, f32[32,2048]{1,0:T(8,128)S(1)}, u32[]{:S(2)}, u32[]{:S(2)}) collective-permute-start(f32[32,2048]{1,0:T(8,128)S(1)} %all_gather.6), channel_id=1, source_target_pairs={{0,4},{4,8},{8,12},{12,16},{16,20},{20,24},{24,28},{28,32},{32,36}... | collective-permute-start | bytes 786440 | tf_op jit(solution)/shard_map/ppermute | solution.py:15
  22.4 1.2 convolution_bitcast_fusion
  23.6 0.8 copy.15
  24.3 0.0 reduce-scatter.4.cloned.1.call-update
  24.3 0.8 fusion.17
  25.1 1.3 fusion.18
  26.5 0.6 compare_and_fusion
  27.1 0.7 compare_and_fusion.1
  27.8 31.8 %reduce-scatter.4.cloned.1.call-done = f32[64,32]{1,0:T(8,128)} async-done(((f32[256,32]{1,0:T(8,128)}), f32[64,32]{1,0:T(8,128)}) %reduce-scatter.4.cloned.1.call-update) | async-done | bytes 8208
  59.6 0.8 copy.16
  60.4 133.4 %all-gather = f32[64,64,32]{1,2,0:T(8,128)S(1)} all-gather(f32[1,64,32]{1,2,0:T(8,128)S(1)} %bitcast.29), channel_id=1, replica_groups=mesh['sub'=64,'blk'=4] {'sub'}, dimensions={0}, use_global_device_ids=true | all-gather | bytes 532480 | tf_op jit(solution)/shard_map/all_gather | solution.py:53
  193.8 0.0 copy-start
  193.8 0.6 copy.14
  194.4 0.4 reshape.35
  194.8 7.4 %fusion.2 = f32[32,256]{1,0:T(8,128)S(1)} fusion(f32[4096,32]{0,1:T(8,128)S(1)} %reshape.35, f32[256,1,4096]{2,1,0:T(1,128)} %param.10), kind=kOutput, calls=%fused_computation.4 | convolution fusion | flops 402653184 | bytes 4751360 | tf_op jit(solution)/shard_map/dot_general | solution.py:52
  202.1 41.3 %psum.7 = f32[32,256]{1,0:T(8,128)S(1)} all-reduce(f32[32,256]{1,0:T(8,128)S(1)} %fusion.2), channel_id=1, replica_groups=mesh['sub'=64,'blk'=4] {'blk'}, use_global_device_ids=true, to_apply=%region_1.3 | all-reduce | flops 8192 | bytes 65536 | tf_op jit(solution)/shard_map/psum | solution.py:59
  243.5 0.0 copy-done
  243.5 0.4 fusion.8
  243.9 0.0 collective-permute-done.1
  243.9 0.3 copy.11
  244.3 0.7 gather_fusion.1
  245.0 0.1 bitcast_select_fusion
  245.1 0.1 copy.13
  245.2 0.0 collective-permute-done
  245.2 0.3 copy.10
  245.5 0.7 gather_fusion
  246.3 0.1 bitcast_select_fusion.1
  246.4 0.1 copy.12
  246.5 6.2 %fusion.5 = f32[32,512]{1,0:T(8,128)} fusion(f32[32,512]{1,0:T(8,128)S(1)} %fusion.8, f32[1,2560,512]{2,1,0:T(8,128)} %param.9, f32[32,256]{1,0:T(8,128)S(1)} %copy.13, f32[32,2048]{1,0:T(8,128)S(1)} %all_gather.6, f32[32,256]{1,0:T(8,128)S(1)} %copy.12), kind=kOutput, calls=%fused_computation.7 | convolution fusion | flops 503496704 | bytes 5701632 | tf_op jit(solution)/shard_map/dot_general | solution.py:38
  (4 shorter events, 0.0 us)
Async XLA Ops:
  6.5 53.0 %reduce-scatter.4.cloned.1.call-start = ((), (), s32[]{:S(2)}) async-start(), calls=%async_computation.1 | async-start | bytes 163840
  17.1 226.9 %collective-permute-start.1 = (f32[32,2048]{1,0:T(8,128)S(1)}, f32[32,2048]{1,0:T(8,128)S(1)}, u32[]{:S(2)}, u32[]{:S(2)}) collective-permute-start(f32[32,2048]{1,0:T(8,128)S(1)} %all_gather.6), channel_id=1, source_target_pairs={{4,0},{8,4},{12,8},{16,12},{20,16},{24,20},{28,24},{32,28},{36,32}... | collective-permute-start | bytes 786440 | tf_op jit(solution)/shard_map/ppermute | solution.py:17
  18.3 226.9 %collective-permute-start = (f32[32,2048]{1,0:T(8,128)S(1)}, f32[32,2048]{1,0:T(8,128)S(1)}, u32[]{:S(2)}, u32[]{:S(2)}) collective-permute-start(f32[32,2048]{1,0:T(8,128)S(1)} %all_gather.6), channel_id=1, source_target_pairs={{0,4},{4,8},{8,12},{12,16},{16,20},{20,24},{24,28},{28,32},{32,36}... | collective-permute-start | bytes 786440 | tf_op jit(solution)/shard_map/ppermute | solution.py:15
  193.8 49.7 %copy-start = (s32[512]{0:T(512)S(1)}, s32[512]{0:T(512)}, u32[]{:S(2)}) copy-start(s32[512]{0:T(512)} %param.13) | copy-start | bytes 6148
Sparse Core Ops, SparseCore 0:
  24.5 35.0 reduce-scatter.3
where the time goes:
time: 260 us
  blocking collectives  185 us (71%)
  waiting for transfers between devices  31.8 us (12%)
  matrix products  15.2 us (6%)
  between operations  13.5 us (5%)
  local copies, waits for them, and re-layouts  6.92 us (3%)
  starting transfers between devices  5.29 us (2%)
    all_gather x1, blocking collectives, on_device(): lax.all_gather(coarse_share, 'sub', axis=1, tiled=True)  133 us
    psum x1, blocking collectives, on_device(): coarse_solution = lax.psum(partial_solution, 'blk')  41.3 us
    unnamed x2, waiting for transfers between devices  31.8 us
    all_gather x1, blocking collectives, on_device(): own_block = lax.all_gather(residual, 'blk', axis=1, tiled=True)  10.5 us
    dot_general x1, matrix products, on_device(): lax.dot_general(lax.all_gather(coarse_share, 'sub', axis=1, tiled=True),...  7.38 us
    dot_general x1, matrix products, on_device(): jnp.dot(extended, fine_inverse[0], precision=lax.Precision.HIGHEST, prefe...  6.2 us
  transfers between devices with their start and end apart: 3, of which 1 were waited for; matrix products, arithmetic and copies ran while one was open for 6% of the time, Pallas kernels for 0%

commit v1 on v0

v1 whole, which is shorter than its diff:
```python
import jax
import jax.numpy as jnp
from jax import lax
from jax.experimental import pallas as pl
from jax.experimental.pallas import tpu as pltpu
from jax.sharding import PartitionSpec as P

NX, NZ, NY = 4, 8, 2
NB = 4
NSUB = NX * NZ * NY
PR = 32
BL = 512
CS = 256
HM = 256
F32, BF16 = jnp.float32, jnp.bfloat16
MESH = pl.DeviceIdType.MESH
Z_ORDER = (0, 1, 7, 2, 6, 3, 5, 4)
NN = (((1,), (0,)), ((), ()))
NT = (((1,), (1,)), ((), ()))


def mm(a, b, dims=NN):
    return lax.dot_general(a, b, dims, preferred_element_type=F32)


def split2(v):
    hi = v.astype(BF16)
    return hi, (v - hi.astype(F32)).astype(BF16)


def split3(v):
    hi = v.astype(BF16)
    rest = v - hi.astype(F32)
    mid = rest.astype(BF16)
    return hi, mid, (rest - mid.astype(F32)).astype(BF16)


def exact(v, onehot, dims=NN):
    n = v.shape[0]
    r = mm(jnp.concatenate(split3(v), axis=0), onehot, dims)
    return (r[:n] + r[n : 2 * n]) + r[2 * n :]


def three(v, w, dims=NN):
    n = v.shape[0]
    vh, vl = split2(v)
    wh, wl = split2(w)
    r = mm(jnp.concatenate([vh, vl], axis=0), wh, dims)
    return (r[:n] + r[n:]) + mm(vh, wl, dims)


def kernel(
    res_ref, agg_ref, want_ref, count_ref, m_hbm, f_hbm, out_ref,
    mbuf, fown, fmar, own, qout, ybuf, xg, nwant, hout, hin, ysum,
    m_sem, f_sem, g_sem, own_s, own_r, y_s, y_r, z_s, z_r, x_s, x_r, w_s, w_r, h_s, h_r, a_s, a_r,
):
    s = lax.axis_index("sub")
    b = lax.axis_index("blk")
    yl = s // (NZ * NX)
    z = lax.rem(s // NX, NZ)
    x = lax.rem(s, NX)
    mate = lax.rem(s + NZ * NX, NSUB)

    def zpos(d):
        return lax.rem(z + d, NZ)

    def at_z(d):
        return yl * (NZ * NX) + zpos(d) * NX + x

    def at_x(d):
        return s - x + lax.rem(x + d, NX)

    def at_b(d):
        return lax.rem(b + d, NB)

    nxt, prv = lax.rem(s + 1, NSUB), lax.rem(s + NSUB - 1, NSUB)

    partners = [(s, at_b(i)) for i in range(1, NB)] + [(mate, at_b(i)) for i in range(NB)]
    partners += [(at_z(d), b) for d in range(1, NZ)] + [(at_x(d), b) for d in range(1, NX)]
    partners += [(nxt, b), (prv, b)]
    barrier = pltpu.get_barrier_semaphore()
    for p in partners:
        pl.semaphore_signal(barrier, inc=1, device_id=p, device_id_type=MESH)

    loads = []
    for i in range(NB):
        rows = pl.ds(pl.multiple_of(HM + at_b(i) * BL, 256), BL)
        loads.append(pltpu.make_async_copy(f_hbm.at[0, rows, :], fown.at[i], f_sem.at[i]))
    for side in range(2):
        rows = pl.ds(side * (HM + NB * BL), HM)
        loads.append(pltpu.make_async_copy(f_hbm.at[0, rows, :], fmar.at[side], g_sem.at[side]))
    mloads = {}
    for k, d in enumerate(Z_ORDER):
        for l in range(NY):
            cols = pl.ds(pl.multiple_of(l * (NZ * CS) + zpos(NZ - d) * CS, 256), CS)
            mloads[k, l] = pltpu.make_async_copy(m_hbm.at[:, 0, cols], mbuf.at[k, l], m_sem.at[k, l])
    loads[0].start()
    for k in range(NZ):
        for l in range(NY):
            mloads[k, l].start()
    for c in loads[1:]:
        c.start()

    low_half = lax.broadcasted_iota(jnp.int32, (PR // 2, 128), 1) < 64

    def halves(even, odd):
        return jnp.where(low_half, even, pltpu.roll(odd, 64, 1)), jnp.where(low_half, pltpu.roll(even, 64, 1), odd)

    onehot = (lax.broadcasted_iota(jnp.int32, (CS, BL), 0) == agg_ref[...]).astype(BF16)
    part = exact(res_ref[...], onehot, NT)
    for h in range(2):
        wide = part[:, h * 128 : (h + 1) * 128]
        even, odd = halves(wide[: PR // 2], wide[PR // 2 :])
        qout[2 * h] = even
        qout[2 * h + 1] = odd

    pl.semaphore_wait(barrier, len(partners))

    def remote(src, dst, ss, rs, to):
        return pltpu.make_async_remote_copy(
            src_ref=src, dst_ref=dst, send_sem=ss, recv_sem=rs, device_id=to, device_id_type=MESH
        )

    sent = []

    def send(*args):
        c = remote(*args)
        c.start()
        sent.append(c)

    ydesc = {}
    for other in range(2):
        for i in range(NB):
            if other or i:
                to = at_b(NB - i)
                args = (qout.at[to], ybuf.at[other, i], y_s.at[other, i], y_r.at[other, i], (mate if other else s, to))
                ydesc[other, i] = args
                send(*args)
    wdesc = [
        (want_ref, nwant.at[0], w_s.at[0], w_r.at[0], (nxt, b)),
        (want_ref, nwant.at[1], w_s.at[1], w_r.at[1], (prv, b)),
    ]
    for args in wdesc:
        send(*args)
    odesc = {}
    for i in range(1, NB):
        args = (res_ref, own.at[i - 1], own_s.at[i], own_r.at[i], (s, at_b(NB - i)))
        odesc[i] = args
        send(*args)

    loads[0].wait()
    fine = three(res_ref[...], fown[0])

    for key in ydesc:
        remote(*ydesc[key]).wait_recv()
    mine = (qout[b] + ybuf[0, 1]) + (ybuf[0, 2] + ybuf[0, 3])
    theirs = (ybuf[1, 0] + ybuf[1, 1]) + (ybuf[1, 2] + ybuf[1, 3])
    slot = z * NX + x
    xg[slot, pl.ds(pl.multiple_of(yl * 16, 16), 16), :] = mine
    xg[slot, pl.ds(pl.multiple_of((1 - yl) * 16, 16), 16), :] = theirs

    def forward(k, d):
        here = zpos(NZ - d) * NX + x
        for e in (1, 3, 2):
            send(xg.at[here], xg.at[here], x_s.at[k, e], x_r.at[k, e], (at_x(e), b))

    for d in Z_ORDER[1:]:
        send(xg.at[slot], xg.at[slot], z_s.at[d], z_r.at[d], (at_z(d), b))
    forward(0, 0)

    for i in range(1, NB):
        loads[i].wait()
        remote(*odesc[i]).wait_recv()
        fine += three(own[i - 1], fown[i])
    for k in (0, 1):
        remote(*wdesc[k]).wait_recv()

    def margin(side):
        wanted = nwant[side, 0, 1 - side : 2 - side, :]
        total = jnp.zeros((PR, HM), F32)
        for i in range(NB):
            rows = lax.broadcasted_iota(jnp.int32, (BL, HM), 0) + at_b(i) * BL
            total += exact(res_ref[...] if i == 0 else own[i - 1], (rows == wanted).astype(BF16))
        hout[side] = total

    hdesc = [
        (hout.at[0], hin.at[1], h_s.at[0], h_r.at[1], (prv, b)),
        (hout.at[1], hin.at[0], h_s.at[1], h_r.at[0], (nxt, b)),
    ]

    def await_z(k):
        d = Z_ORDER[k]
        here = xg.at[zpos(NZ - d) * NX + x]
        remote(here, here, z_s.at[d], z_r.at[d], (at_z(d), b)).wait_recv()
        forward(k, d)

    def product(k):
        d = Z_ORDER[k]
        base = zpos(NZ - d) * NX
        for e in (1, 3, 2):
            there = xg.at[base + lax.rem(x + NX - e, NX)]
            remote(there, there, x_s.at[k, e], x_r.at[k, e], (at_x(e), b)).wait_recv()
        total = None
        for l in range(NY):
            cols = []
            for h in range(2):
                even = xg[base + 2 * h, 16 * l : 16 * l + 16, :]
                odd = xg[base + 2 * h + 1, 16 * l : 16 * l + 16, :]
                top, bottom = halves(even, odd)
                cols.append(jnp.concatenate([top, bottom], axis=0))
            mloads[k, l].wait()
            r = three(jnp.concatenate(cols, axis=1), mbuf[k, l], NT)
            total = r if total is None else total + r
        return total

    await_z(1)
    await_z(2)
    margin(0)
    send(*hdesc[0])
    await_z(3)
    await_z(4)
    margin(1)
    send(*hdesc[1])
    await_z(5)
    await_z(6)
    coarse = product(0)
    await_z(7)
    for k in range(1, NZ):
        coarse += product(k)

    ysum[0] = coarse
    adesc = {}
    for i in range(1, NB):
        args = (ysum.at[0], ysum.at[i], a_s.at[i], a_r.at[i], (s, at_b(NB - i)))
        adesc[i] = args
        send(*args)

    slots = lax.broadcasted_iota(jnp.int32, (PR, HM), 1)
    for side in range(2):
        remote(*hdesc[1 - side]).wait_recv()
        edge = s == (0 if side == 0 else NSUB - 1)
        kept = jnp.where(edge, 0, count_ref[0, side])
        loads[NB + side].wait()
        fine += three(jnp.where(slots < kept, hin[side], 0.0), fmar[side])

    for i in range(1, NB):
        remote(*adesc[i]).wait_recv()
    coarse = (ysum[0] + ysum[1]) + (ysum[2] + ysum[3])
    out_ref[...] = fine + exact(coarse, onehot)
    for c in sent:
        c.wait_send()


def on_device(residual, fine_inverse, coarse_inverse, wanted_rows, wanted_count, aggregate):
    vmem = pl.BlockSpec(memory_space=pltpu.VMEM)
    hbm = pl.BlockSpec(memory_space=pltpu.HBM)
    dma = pltpu.SemaphoreType.DMA
    return pl.pallas_call(
        kernel,
        out_shape=jax.ShapeDtypeStruct((PR, BL), F32),
        in_specs=[vmem, vmem, vmem, pl.BlockSpec(memory_space=pltpu.SMEM), hbm, hbm],
        out_specs=vmem,
        scratch_shapes=[
            pltpu.VMEM((NZ, NY, CS, CS), F32),
            pltpu.VMEM((NB, BL, BL), F32),
            pltpu.VMEM((2, HM, BL), F32),
            pltpu.VMEM((NB - 1, PR, BL), F32),
            pltpu.VMEM((NB, PR // 2, 128), F32),
            pltpu.VMEM((2, NB, PR // 2, 128), F32),
            pltpu.VMEM((NZ * NX, PR, 128), F32),
            pltpu.VMEM((2, 1, 2, HM), jnp.int32),
            pltpu.VMEM((2, PR, HM), F32),
            pltpu.VMEM((2, PR, HM), F32),
            pltpu.VMEM((NB, PR, CS), F32),
            dma((NZ, NY)), dma((NB,)), dma((2,)),
            dma((NB,)), dma((NB,)),
            dma((2, NB)), dma((2, NB)),
            dma((NZ,)), dma((NZ,)),
            dma((NZ, NX)), dma((NZ, NX)),
            dma((2,)), dma((2,)),
            dma((2,)), dma((2,)),
            dma((NB,)), dma((NB,)),
        ],
        compiler_params=pltpu.CompilerParams(
            collective_id=0, has_side_effects=True, vmem_limit_bytes=48 * 1024 * 1024
        ),
        name="schwarz",
    )(residual, aggregate.reshape(1, BL), wanted_rows, wanted_count, coarse_inverse, fine_inverse)


def solution(mesh):
    in_specs = (
        P(None, ("sub", "blk")),
        P("sub", None, "blk"),
        P("sub", "blk", None),
        P("sub", None, None),
        P("sub", None),
        P(("sub", "blk")),
    )
    out_specs = P(None, ("sub", "blk"))
    return jax.shard_map(
        on_device, mesh=mesh, in_specs=in_specs, out_specs=out_specs, check_vma=False
    )
```

time: 260 us -> 37.8 us (0.15)
  blocking collectives: 185 us -> 0 us
  Pallas kernels: 0 us -> 31.9 us
  waiting for transfers between devices: 31.8 us -> 0 us
  matrix products: 15.2 us -> 0 us
  between operations: 13.5 us -> 0.01 us
  starting transfers between devices: 5.29 us -> 0 us
    all_gather x2 -> x0, blocking collectives: 144 us -> none  [the longest x1 133 us: on_device(): lax.all_gather(coarse_share, 'sub', axis=1, tiled=True)]
    psum x1 -> x0, blocking collectives: 41.3 us -> none  [on_device(): coarse_solution = lax.psum(partial_solution, 'blk')]
    pallas_call x0 -> x1, Pallas kernels: none -> 31.9 us  [on_device(): pl.pallas_call(kernel, out_shape=jax.ShapeDtypeStruct((PR, BL), F32), in_...]
    unnamed x2 -> x0, waiting for transfers between devices: 31.8 us -> none
    dot_general x4 -> x0, matrix products: 15.2 us -> none  [the longest x1 7.38 us: on_device(): lax.dot_general(lax.all_gather(coarse_share, 'sub', axis=1, tiled=True),...]
    ppermute x2 -> x0, starting transfers between devices: 5.28 us -> none  [the longest x1 4 us: with_halo(): lax.ppermute(tail, axis, [(i, (i + 1) % count) for i in range(ends)])]
    unnamed x5 -> x11, local copies, waits for them, and re-layouts: 1.94 us -> 5.68 us
  transfers between devices with their start and end apart: 3 -> 0, of which waited for: 1 -> 0; matrix products, arithmetic and copies ran while one was open for 6% -> 0% of each run, Pallas kernels for 0% -> 0%
where the time goes in v1:
time: 37.8 us; the launch traced here: 37.6 us
  Pallas kernels  31.9 us (84%)
  local copies, waits for them, and re-layouts  5.68 us (15%)
    pallas_call x1, Pallas kernels, on_device(): pl.pallas_call(kernel, out_shape=jax.ShapeDtypeStruct((PR, BL), F32), in_...  31.9 us
    unnamed x11, local copies, waits for them, and re-layouts  5.68 us

profile of v1, /device:TPU:1, one launch (start us, length us, event | category | flops | bytes accessed | tf_op | source)
XLA Modules:
  0.0 37.6 jit_solution(2543756945684285175)
XLA Ops:
  0.0 0.0 copy-start
  0.0 2.2 %copy-done = f32[256,1,4096]{2,1,0:T(1,128)S(1)} copy-done((f32[256,1,4096]{2,1,0:T(1,128)S(1)}, f32[256,1,4096]{2,1,0:T(1,128)}, u32[]{:S(2)}) %copy-start) | copy-done | bytes 4194328
  2.2 0.0 copy-start.1
  2.2 0.8 %copy-done.1 = f32[32,512]{1,0:T(8,128)S(1)} copy-done((f32[32,512]{1,0:T(8,128)S(1)}, f32[32,512]{1,0:T(8,128)}, u32[]{:S(2)}) %copy-start.1) | copy-done | bytes 65560
  3.0 0.0 copy-start.2
  3.0 0.7 %copy-done.2 = s32[512]{0:T(512)S(1)} copy-done((s32[512]{0:T(512)S(1)}, s32[512]{0:T(512)}, u32[]{:S(2)}) %copy-start.2) | copy-done | bytes 2072
  3.7 0.0 copy-start.3
  3.7 0.7 %copy-done.3 = s32[1,2,256]{2,1,0:T(2,128)S(1)} copy-done((s32[1,2,256]{2,1,0:T(2,128)S(1)}, s32[1,2,256]{2,1,0:T(2,128)}, u32[]{:S(2)}) %copy-start.3) | copy-done | bytes 2072
  4.4 0.0 copy-start.4
  4.4 0.7 %copy-done.4 = s32[1,2]{1,0:T(1,128)S(1)} copy-done((s32[1,2]{1,0:T(1,128)S(1)}, s32[1,2]{1,0:T(1,128)}, u32[]{:S(2)}) %copy-start.4) | copy-done | bytes 32
  5.0 31.9 %schwarz.1 = f32[32,512]{1,0:T(8,128)S(1)} custom-call(f32[32,512]{1,0:T(8,128)S(1)} %copy-done.1, s32[1,512]{1,0:T(1,128)S(1)} %bitcast.1, s32[1,2,256]{2,1,0:T(2,128)S(1)} %copy-done.3, s32[1,2]{1,0:T(1,128)S(1)} %copy-done.4, f32[256,1,4096]{2,1,0:T(1,128)S(1)} %copy-done, f32[1,2560,512]{2,1,0:T(8,128)} %f_hbm.1), custom_call_target="tpu_custom_call" | custom-call | tf_op jit(solution)/shard_map/schwarz/pallas_call | solution.py:258
  37.0 0.6 %copy.8 = f32[32,512]{1,0:T(8,128)} copy(f32[32,512]{1,0:T(8,128)S(1)} %schwarz.1) | data formatting | bytes 131072
Async XLA Ops:
  0.0 2.2 %copy-start = (f32[256,1,4096]{2,1,0:T(1,128)S(1)}, f32[256,1,4096]{2,1,0:T(1,128)}, u32[]{:S(2)}) copy-start(f32[256,1,4096]{2,1,0:T(1,128)} %m_hbm.1) | copy-start | bytes 12582916
  2.2 0.8 %copy-start.1 = (f32[32,512]{1,0:T(8,128)S(1)}, f32[32,512]{1,0:T(8,128)}, u32[]{:S(2)}) copy-start(f32[32,512]{1,0:T(8,128)} %res_ref.1) | copy-start | bytes 196612
  3.0 0.7 %copy-start.2 = (s32[512]{0:T(512)S(1)}, s32[512]{0:T(512)}, u32[]{:S(2)}) copy-start(s32[512]{0:T(512)} %param.11) | copy-start | bytes 6148
  3.7 0.7 %copy-start.3 = (s32[1,2,256]{2,1,0:T(2,128)S(1)}, s32[1,2,256]{2,1,0:T(2,128)}, u32[]{:S(2)}) copy-start(s32[1,2,256]{2,1,0:T(2,128)} %want_ref.1) | copy-start | bytes 6148
  4.4 0.7 %copy-start.4 = (s32[1,2]{1,0:T(1,128)S(1)}, s32[1,2]{1,0:T(1,128)}, u32[]{:S(2)}) copy-start(s32[1,2]{1,0:T(1,128)} %count_ref.1) | copy-start | bytes 28

commit v2 on v1

v2 whole, which is shorter than its diff:
```python
import jax
import jax.numpy as jnp
from jax import lax
from jax.experimental import pallas as pl
from jax.experimental.pallas import tpu as pltpu
from jax.sharding import PartitionSpec as P

NX, NZ, NY = 4, 8, 2
NB = 4
NSUB = NX * NZ * NY
PR = 32
BL = 512
CS = 256
HM = 256
F32, BF16 = jnp.float32, jnp.bfloat16
MESH = pl.DeviceIdType.MESH
Z_ORDER = (0, 1, 7, 2, 6, 3, 5, 4)
NEAR = (1, 7, 2, 6)
NN = (((1,), (0,)), ((), ()))
NT = (((1,), (1,)), ((), ()))


def mm(a, b, dims=NN):
    return lax.dot_general(a, b, dims, preferred_element_type=F32)


def split2(v):
    hi = v.astype(BF16)
    return hi, (v - hi.astype(F32)).astype(BF16)


def split3(v):
    hi = v.astype(BF16)
    rest = v - hi.astype(F32)
    mid = rest.astype(BF16)
    return hi, mid, (rest - mid.astype(F32)).astype(BF16)


def exact(v, onehot, dims=NN):
    n = v.shape[0]
    r = mm(jnp.concatenate(split3(v), axis=0), onehot, dims)
    return (r[:n] + r[n : 2 * n]) + r[2 * n :]


def three(v, w, dims=NN):
    n = v.shape[0]
    vh, vl = split2(v)
    wh, wl = split2(w)
    r = mm(jnp.concatenate([vh, vl], axis=0), wh, dims)
    return (r[:n] + r[n:]) + mm(vh, wl, dims)


def kernel(
    res_hbm, agg_hbm, want_hbm, count_hbm, m_hbm, f_hbm, out_ref,
    res_ref, agg_ref, want_ref, count_ref, mbuf, fown, fmar, own, qout, ybuf, xg, nwant, hout, hin, ysum,
    i_sem, m_sem, f_sem, g_sem, own_s, own_r, y_s, y_r, z_s, z_r, v_s, v_r, x_s, x_r, w_s, w_r, h_s, h_r, a_s, a_r, far,
):
    s = lax.axis_index("sub")
    b = lax.axis_index("blk")
    yl = s // (NZ * NX)
    z = lax.rem(s // NX, NZ)
    x = lax.rem(s, NX)
    mate = lax.rem(s + NZ * NX, NSUB)

    def zpos(d):
        return lax.rem(z + d, NZ)

    def at_z(d):
        return yl * (NZ * NX) + zpos(d) * NX + x

    def at_x(d):
        return s - x + lax.rem(x + d, NX)

    at_b = (b, b + 1 - 2 * lax.rem(b, 2), lax.rem(b + 2, NB), NB - 1 - b)
    nxt, prv = lax.rem(s + 1, NSUB), lax.rem(s + NSUB - 1, NSUB)

    partners = [(s, at_b[i]) for i in (2, 3, 1)] + [(mate, at_b[i]) for i in range(NB)]
    partners += [(at_z(d), b) for d in (2, 6, 1, 7)] + [(at_x(d), b) for d in (2, 1, 3)]
    partners += [(nxt, b), (prv, b)]
    barrier = pltpu.get_barrier_semaphore()
    for p in partners:
        pl.semaphore_signal(barrier, inc=1, device_id=p, device_id_type=MESH)

    inputs = [
        pltpu.make_async_copy(src, dst, i_sem.at[i])
        for i, (src, dst) in enumerate(
            [(res_hbm, res_ref), (agg_hbm, agg_ref), (want_hbm, want_ref), (count_hbm, count_ref)]
        )
    ]
    for c in inputs:
        c.start()

    loads = []
    for i in range(NB):
        rows = pl.ds(pl.multiple_of(HM + at_b[i] * BL, 256), BL)
        loads.append(pltpu.make_async_copy(f_hbm.at[0, rows, :], fown.at[i], f_sem.at[i]))
    for side in range(2):
        rows = pl.ds(side * (HM + NB * BL), HM)
        loads.append(pltpu.make_async_copy(f_hbm.at[0, rows, :], fmar.at[side], g_sem.at[side]))
    mloads = {}
    for d in Z_ORDER:
        for l in range(NY):
            cols = pl.ds(pl.multiple_of(l * (NZ * CS) + zpos(NZ - d) * CS, 256), CS)
            mloads[d, l] = pltpu.make_async_copy(m_hbm.at[:, 0, cols], mbuf.at[d, l], m_sem.at[d, l])
    loads[0].start()
    for c in mloads.values():
        c.start()
    for c in loads[1:]:
        c.start()

    low_half = lax.broadcasted_iota(jnp.int32, (PR // 2, 128), 1) < 64

    def halves(even, odd):
        return jnp.where(low_half, even, pltpu.roll(odd, 64, 1)), jnp.where(low_half, pltpu.roll(even, 64, 1), odd)

    inputs[0].wait()
    inputs[1].wait()
    onehot = (lax.broadcasted_iota(jnp.int32, (CS, BL), 0) == agg_ref[...]).astype(BF16)
    part = exact(res_ref[...], onehot, NT)
    for h in range(2):
        wide = part[:, h * 128 : (h + 1) * 128]
        even, odd = halves(wide[: PR // 2], wide[PR // 2 :])
        qout[2 * h] = even
        qout[2 * h + 1] = odd

    pl.semaphore_wait(barrier, len(partners))

    def remote(src, dst, ss, rs, to):
        return pltpu.make_async_remote_copy(
            src_ref=src, dst_ref=dst, send_sem=ss, recv_sem=rs, device_id=to, device_id_type=MESH
        )

    sent = []

    def send(*args):
        c = remote(*args)
        c.start()
        sent.append(c)

    ydesc = []
    for other, i in ((0, 2), (0, 3), (1, 0), (1, 1), (1, 2), (1, 3), (0, 1)):
        to = at_b[i]
        ydesc.append((qout.at[to], ybuf.at[other, i], y_s.at[other, i], y_r.at[other, i], (mate if other else s, to)))
        send(*ydesc[-1])
    for d in (2, 6):
        pl.semaphore_signal(far, inc=1, device_id=(at_z(d), b), device_id_type=MESH)
    inputs[2].wait()
    wdesc = [
        (want_ref, nwant.at[0], w_s.at[0], w_r.at[0], (nxt, b)),
        (want_ref, nwant.at[1], w_s.at[1], w_r.at[1], (prv, b)),
    ]
    for args in wdesc:
        send(*args)

    loads[0].wait()
    fine = three(res_ref[...], fown[0])

    for args in ydesc:
        remote(*args).wait_recv()
    mine = (qout[b] + ybuf[0, 1]) + (ybuf[0, 2] + ybuf[0, 3])
    theirs = (ybuf[1, 0] + ybuf[1, 1]) + (ybuf[1, 2] + ybuf[1, 3])
    slot = z * NX + x
    xg[slot, pl.ds(pl.multiple_of(yl * 16, 16), 16), :] = mine
    xg[slot, pl.ds(pl.multiple_of((1 - yl) * 16, 16), 16), :] = theirs

    def slot_of(d, e):
        return zpos(NZ - d) * NX + lax.rem(x + NX - e, NX)

    def to_z(d, e, ss, rs):
        here = xg.at[z * NX + lax.rem(x + NX - e, NX)]
        send(here, here, ss.at[d], rs.at[d], (at_z(d), b))

    def to_x(d):
        here = xg.at[slot_of(d, 0)]
        for e in (1, 3) if d in NEAR else (2, 1, 3):
            send(here, here, x_s.at[d, e], x_r.at[d, e], (at_x(e), b))

    def await_block(d, e, ss, rs):
        there = xg.at[slot_of(d, e)]
        remote(there, there, ss, rs, (s, at_b[1])).wait_recv()

    def await_z(*ds):
        for d in ds:
            await_block(d, 0, z_s.at[d], z_r.at[d])
            to_x(d)

    for d in (1, 7):
        to_z(d, 0, z_s, z_r)
    to_x(0)
    for d in (2, 6):
        to_z(d, 0, z_s, z_r)
    pl.semaphore_wait(far, 2)
    for d in (4, 3, 5):
        to_z(d, 0, z_s, z_r)
    odesc = {}
    for i in (2, 3, 1):
        odesc[i] = (res_ref, own.at[i - 1], own_s.at[i], own_r.at[i], (s, at_b[i]))
        send(*odesc[i])

    await_z(1, 7)
    await_z(2, 6)
    await_block(0, 2, x_s.at[0, 2], x_r.at[0, 2])
    for d in NEAR:
        to_z(d, 2, v_s, v_r)
    await_z(3, 5)
    await_z(4)

    def products(*ds):
        for d in ds:
            for e in (1, 3) if d in NEAR else (1, 3) if d == 0 else (1, 3, 2):
                await_block(d, e, x_s.at[d, e], x_r.at[d, e])
            if d in NEAR:
                await_block(d, 2, v_s.at[d], v_r.at[d])
            for l in range(NY):
                mloads[d, l].wait()
        total = None
        for d in ds:
            base = zpos(NZ - d) * NX
            for l in range(NY):
                cols = []
                for h in range(2):
                    even = xg[base + 2 * h, 16 * l : 16 * l + 16, :]
                    odd = xg[base + 2 * h + 1, 16 * l : 16 * l + 16, :]
                    cols.append(jnp.concatenate(halves(even, odd), axis=0))
                r = three(jnp.concatenate(cols, axis=1), mbuf[d, l], NT)
                total = r if total is None else total + r
        return total

    coarse = products(0, 1, 7)
    coarse += products(2, 6)

    for i in (2, 3, 1):
        remote(*odesc[i]).wait_recv()
    for args in wdesc:
        remote(*args).wait_recv()
    hdesc = [
        (hout.at[0], hin.at[1], h_s.at[0], h_r.at[1], (prv, b)),
        (hout.at[1], hin.at[0], h_s.at[1], h_r.at[0], (nxt, b)),
    ]
    for side in range(2):
        wanted = nwant[side, 0, 1 - side : 2 - side, :]
        total = None
        for i in range(NB):
            rows = lax.broadcasted_iota(jnp.int32, (BL, HM), 0) + at_b[i] * BL
            r = exact(res_ref[...] if i == 0 else own[i - 1], (rows == wanted).astype(BF16))
            total = r if total is None else total + r
        hout[side] = total
    for args in hdesc:
        send(*args)

    coarse += products(3, 5, 4)
    ysum[0] = coarse
    adesc = {}
    for i in (2, 3, 1):
        adesc[i] = (ysum.at[0], ysum.at[i], a_s.at[i], a_r.at[i], (s, at_b[i]))
        send(*adesc[i])

    for i in range(1, NB):
        loads[i].wait()
    for i in range(1, NB):
        fine += three(own[i - 1], fown[i])
    inputs[3].wait()
    slots = lax.broadcasted_iota(jnp.int32, (PR, HM), 1)
    for side in range(2):
        remote(*hdesc[1 - side]).wait_recv()
        loads[NB + side].wait()
    for side in range(2):
        edge = s == (0 if side == 0 else NSUB - 1)
        kept = jnp.where(edge, 0, count_ref[0, side])
        fine += three(jnp.where(slots < kept, hin[side], 0.0), fmar[side])

    for i in (1, 2, 3):
        remote(*adesc[i]).wait_recv()
    coarse = (ysum[0] + ysum[1]) + (ysum[2] + ysum[3])
    out_ref[...] = fine + exact(coarse, onehot)
    for c in sent:
        c.wait_send()


def on_device(residual, fine_inverse, coarse_inverse, wanted_rows, wanted_count, aggregate):
    vmem = pl.BlockSpec(memory_space=pltpu.VMEM)
    hbm = pl.BlockSpec(memory_space=pl.ANY)
    dma = pltpu.SemaphoreType.DMA
    return pl.pallas_call(
        kernel,
        out_shape=jax.ShapeDtypeStruct((PR, BL), F32),
        in_specs=[hbm] * 6,
        out_specs=vmem,
        scratch_shapes=[
            pltpu.VMEM((PR, BL), F32),
            pltpu.VMEM((1, BL), jnp.int32),
            pltpu.VMEM((1, 2, HM), jnp.int32),
            pltpu.SMEM((1, 2), jnp.int32),
            pltpu.VMEM((NZ, NY, CS, CS), F32),
            pltpu.VMEM((NB, BL, BL), F32),
            pltpu.VMEM((2, HM, BL), F32),
            pltpu.VMEM((NB - 1, PR, BL), F32),
            pltpu.VMEM((NB, PR // 2, 128), F32),
            pltpu.VMEM((2, NB, PR // 2, 128), F32),
            pltpu.VMEM((NZ * NX, PR, 128), F32),
            pltpu.VMEM((2, 1, 2, HM), jnp.int32),
            pltpu.VMEM((2, PR, HM), F32),
            pltpu.VMEM((2, PR, HM), F32),
            pltpu.VMEM((NB, PR, CS), F32),
            dma((4,)), dma((NZ, NY)), dma((NB,)), dma((2,)),
            dma((NB,)), dma((NB,)),
            dma((2, NB)), dma((2, NB)),
            dma((NZ,)), dma((NZ,)),
            dma((NZ,)), dma((NZ,)),
            dma((NZ, NX)), dma((NZ, NX)),
            dma((2,)), dma((2,)),
            dma((2,)), dma((2,)),
            dma((NB,)), dma((NB,)),
            pltpu.SemaphoreType.REGULAR,
        ],
        compiler_params=pltpu.CompilerParams(
            collective_id=0, has_side_effects=True, vmem_limit_bytes=48 * 1024 * 1024
        ),
        name="schwarz",
    )(*[pltpu.with_memory_space_constraint(v, pltpu.HBM) for v in (residual, aggregate.reshape(1, BL), wanted_rows, wanted_count, coarse_inverse, fine_inverse)])


def solution(mesh):
    in_specs = (
        P(None, ("sub", "blk")),
        P("sub", None, "blk"),
        P("sub", "blk", None),
        P("sub", None, None),
        P("sub", None),
        P(("sub", "blk")),
    )
    out_specs = P(None, ("sub", "blk"))
    return jax.shard_map(
        on_device, mesh=mesh, in_specs=in_specs, out_specs=out_specs, check_vma=False
    )
```

time: 37.8 us -> 31 us (0.82)
  local copies, waits for them, and re-layouts: 5.68 us -> 0.63 us
  Pallas kernels: 31.9 us -> 30.3 us
    unnamed x11 -> x1, local copies, waits for them, and re-layouts: 5.68 us -> 0.63 us
    pallas_call x1, Pallas kernels: 31.9 us -> 30.3 us  [on_device(): pl.pallas_call(kernel, out_shape=jax.ShapeDtypeStruct((PR, BL), F32), in_...]
where the time goes in v2:
time: 31 us
  Pallas kernels  30.3 us (98%)
  local copies, waits for them, and re-layouts  0.63 us (2%)
    pallas_call x1, Pallas kernels, on_device(): pl.pallas_call(kernel, out_shape=jax.ShapeDtypeStruct((PR, BL), F32), in_...  30.3 us
    unnamed x1, local copies, waits for them, and re-layouts  0.63 us

profile of v2, /device:TPU:1, one launch (start us, length us, event | category | flops | bytes accessed | tf_op | source)
XLA Modules:
  0.0 31.0 jit_solution(10981508744990946587)
XLA Ops:
  0.0 30.3 %schwarz.1 = f32[32,512]{1,0:T(8,128)S(1)} custom-call(f32[32,512]{1,0:T(8,128)} %res_hbm.1, s32[1,512]{1,0:T(1,128)} %bitcast.1, s32[1,2,256]{2,1,0:T(2,128)} %want_hbm.1, s32[1,2]{1,0:T(1,128)} %count_hbm.1, f32[256,1,4096]{2,1,0:T(1,128)} %m_hbm.1, f32[1,2560,512]{2,1,0:T(8,128)} %f_hbm.1), custom_call_target="tpu_custom_call" | custom-call | tf_op jit(solution)/shard_map/schwarz/pallas_call | solution.py:284
  30.3 0.6 %copy.8 = f32[32,512]{1,0:T(8,128)} copy(f32[32,512]{1,0:T(8,128)S(1)} %schwarz.1) | data formatting | bytes 131072

commit v3 on v2

--- a/solution.py
+++ b/solution.py
@@ -14,8 +14,8 @@
 HM = 256
 F32, BF16 = jnp.float32, jnp.bfloat16
 MESH = pl.DeviceIdType.MESH
-Z_ORDER = (0, 1, 7, 2, 6, 3, 5, 4)
-NEAR = (1, 7, 2, 6)
+EARLY, LATE = (0, 1, 2, 3), (7, 6, 5, 4)
+NEAR = (1, 2, 7, 6)
 NN = (((1,), (0,)), ((), ()))
 NT = (((1,), (1,)), ((), ()))
 
@@ -53,7 +53,7 @@
 def kernel(
     res_hbm, agg_hbm, want_hbm, count_hbm, m_hbm, f_hbm, out_ref,
     res_ref, agg_ref, want_ref, count_ref, mbuf, fown, fmar, own, qout, ybuf, xg, nwant, hout, hin, ysum,
-    i_sem, m_sem, f_sem, g_sem, own_s, own_r, y_s, y_r, z_s, z_r, v_s, v_r, x_s, x_r, w_s, w_r, h_s, h_r, a_s, a_r, far,
+    i_sem, m_sem, f_sem, g_sem, own_s, own_r, y_s, y_r, z_s, z_r, v_s, o_r, x_s, x_r, w_s, w_r, h_s, h_r, a_s, a_r, z_in, s_in,
 ):
     s = lax.axis_index("sub")
     b = lax.axis_index("blk")
@@ -73,13 +73,6 @@
 
     at_b = (b, b + 1 - 2 * lax.rem(b, 2), lax.rem(b + 2, NB), NB - 1 - b)
     nxt, prv = lax.rem(s + 1, NSUB), lax.rem(s + NSUB - 1, NSUB)
-
-    partners = [(s, at_b[i]) for i in (2, 3, 1)] + [(mate, at_b[i]) for i in range(NB)]
-    partners += [(at_z(d), b) for d in (2, 6, 1, 7)] + [(at_x(d), b) for d in (2, 1, 3)]
-    partners += [(nxt, b), (prv, b)]
-    barrier = pltpu.get_barrier_semaphore()
-    for p in partners:
-        pl.semaphore_signal(barrier, inc=1, device_id=p, device_id_type=MESH)
 
     inputs = [
         pltpu.make_async_copy(src, dst, i_sem.at[i])
@@ -90,23 +83,33 @@
     for c in inputs:
         c.start()
 
-    loads = []
-    for i in range(NB):
-        rows = pl.ds(pl.multiple_of(HM + at_b[i] * BL, 256), BL)
-        loads.append(pltpu.make_async_copy(f_hbm.at[0, rows, :], fown.at[i], f_sem.at[i]))
-    for side in range(2):
-        rows = pl.ds(side * (HM + NB * BL), HM)
-        loads.append(pltpu.make_async_copy(f_hbm.at[0, rows, :], fmar.at[side], g_sem.at[side]))
-    mloads = {}
-    for d in Z_ORDER:
-        for l in range(NY):
-            cols = pl.ds(pl.multiple_of(l * (NZ * CS) + zpos(NZ - d) * CS, 256), CS)
-            mloads[d, l] = pltpu.make_async_copy(m_hbm.at[:, 0, cols], mbuf.at[d, l], m_sem.at[d, l])
-    loads[0].start()
-    for c in mloads.values():
-        c.start()
-    for c in loads[1:]:
-        c.start()
+    def along_z(zp):
+        return (yl * (NZ * NX) + zp * NX + x, b)
+
+    cross_next, cross_prev = x == NX - 1, x == 0
+    barrier = pltpu.get_barrier_semaphore()
+
+    def signal(sem, to):
+        pl.semaphore_signal(sem, inc=1, device_id=to, device_id_type=MESH)
+
+    level = [(s, at_b[i]) for i in (2, 3, 1)] + [(mate, at_b[i]) for i in range(NB)] + [(at_x(d), b) for d in (2, 1, 3)]
+    for p in level:
+        signal(barrier, p)
+    for zp in range(1, NZ):
+        @pl.when(zp > z)
+        def _():
+            signal(barrier, along_z(zp))
+
+    @pl.when(cross_next & (z < NZ - 1))
+    def _():
+        signal(barrier, (nxt, b))
+
+    @pl.when(cross_prev & (z == 0))
+    def _():
+        signal(barrier, (prv, b))
+
+    answers_prev, answers_next = cross_prev & (z > 0), cross_next & (z == NZ - 1)
+    greeted = len(level) + z + jnp.where(answers_prev | answers_next, 1, 0)
 
     low_half = lax.broadcasted_iota(jnp.int32, (PR // 2, 128), 1) < 64
 
@@ -123,7 +126,7 @@
         qout[2 * h] = even
         qout[2 * h + 1] = odd
 
-    pl.semaphore_wait(barrier, len(partners))
+    pl.semaphore_wait(barrier, greeted)
 
     def remote(src, dst, ss, rs, to):
         return pltpu.make_async_remote_copy(
@@ -142,16 +145,34 @@
         to = at_b[i]
         ydesc.append((qout.at[to], ybuf.at[other, i], y_s.at[other, i], y_r.at[other, i], (mate if other else s, to)))
         send(*ydesc[-1])
-    for d in (2, 6):
-        pl.semaphore_signal(far, inc=1, device_id=(at_z(d), b), device_id_type=MESH)
-    inputs[2].wait()
-    wdesc = [
-        (want_ref, nwant.at[0], w_s.at[0], w_r.at[0], (nxt, b)),
-        (want_ref, nwant.at[1], w_s.at[1], w_r.at[1], (prv, b)),
-    ]
-    for args in wdesc:
-        send(*args)
-
+    for zp in range(NZ - 1):
+        @pl.when(zp < z)
+        def _():
+            signal(z_in.at[z], along_z(zp))
+
+    @pl.when(answers_prev)
+    def _():
+        signal(s_in, (prv, b))
+
+    @pl.when(answers_next)
+    def _():
+        signal(s_in, (nxt, b))
+
+    loads = []
+    for i in range(NB):
+        rows = pl.ds(pl.multiple_of(HM + at_b[i] * BL, 256), BL)
+        loads.append(pltpu.make_async_copy(f_hbm.at[0, rows, :], fown.at[i], f_sem.at[i]))
+    for side in range(2):
+        rows = pl.ds(side * (HM + NB * BL), HM)
+        loads.append(pltpu.make_async_copy(f_hbm.at[0, rows, :], fmar.at[side], g_sem.at[side]))
+    for c in loads:
+        c.start()
+    mloads = {}
+    for zp in range(NZ):
+        for l in range(NY):
+            cols = pl.ds(l * (NZ * CS) + zp * CS, CS)
+            mloads[zp, l] = pltpu.make_async_copy(m_hbm.at[:, 0, cols], mbuf.at[zp, l], m_sem.at[zp, l])
+            mloads[zp, l].start()
     loads[0].wait()
     fine = three(res_ref[...], fown[0])
 
@@ -163,81 +184,78 @@
     xg[slot, pl.ds(pl.multiple_of(yl * 16, 16), 16), :] = mine
     xg[slot, pl.ds(pl.multiple_of((1 - yl) * 16, 16), 16), :] = theirs
 
-    def slot_of(d, e):
-        return zpos(NZ - d) * NX + lax.rem(x + NX - e, NX)
-
-    def to_z(d, e, ss, rs):
-        here = xg.at[z * NX + lax.rem(x + NX - e, NX)]
-        send(here, here, ss.at[d], rs.at[d], (at_z(d), b))
-
-    def to_x(d):
-        here = xg.at[slot_of(d, 0)]
-        for e in (1, 3) if d in NEAR else (2, 1, 3):
-            send(here, here, x_s.at[d, e], x_r.at[d, e], (at_x(e), b))
-
-    def await_block(d, e, ss, rs):
-        there = xg.at[slot_of(d, e)]
-        remote(there, there, ss, rs, (s, at_b[1])).wait_recv()
-
-    def await_z(*ds):
-        for d in ds:
-            await_block(d, 0, z_s.at[d], z_r.at[d])
-            to_x(d)
-
-    for d in (1, 7):
-        to_z(d, 0, z_s, z_r)
-    to_x(0)
-    for d in (2, 6):
-        to_z(d, 0, z_s, z_r)
-    pl.semaphore_wait(far, 2)
-    for d in (4, 3, 5):
-        to_z(d, 0, z_s, z_r)
+    def block(zp, e):
+        return xg.at[zp * NX + lax.rem(x + NX - e, NX)]
+
+    def near(zp):
+        d = lax.rem(z + NZ - zp, NZ)
+        return (d == 1) | (d == 2) | (d == 6) | (d == 7)
+
+    def z_copy(zp):
+        return remote(block(z, 0), block(z, 0), z_s.at[zp], z_r.at[z], along_z(zp))
+
+    def v_copy(d):
+        return remote(block(z, 2), block(z, 2), v_s.at[d], o_r.at[z], (at_z(d), b))
+
+    def x_copy(zp, e):
+        rs = o_r.at[zp] if e == 2 else x_r.at[zp, e]
+        return remote(block(zp, 0), block(zp, 0), x_s.at[zp, e], rs, (at_x(e), b))
+
+    def arrival(zp, e, rs):
+        remote(block(zp, e), block(zp, e), x_s.at[0, 0], rs, (s, at_b[1])).wait_recv()
+
+    def forward(zp):
+        @pl.when(zp != z)
+        def _():
+            arrival(zp, 0, z_r.at[zp])
+
+            @pl.when(jnp.logical_not(near(zp)))
+            def _():
+                x_copy(zp, 2).start()
+
+            x_copy(zp, 1).start()
+            x_copy(zp, 3).start()
+
+    for zp in range(NZ - 1):
+        @pl.when(zp < z)
+        def _():
+            z_copy(zp).start()
+    for e in (2, 1, 3):
+        x_copy(z, e).start()
     odesc = {}
     for i in (2, 3, 1):
         odesc[i] = (res_ref, own.at[i - 1], own_s.at[i], own_r.at[i], (s, at_b[i]))
         send(*odesc[i])
-
-    await_z(1, 7)
-    await_z(2, 6)
-    await_block(0, 2, x_s.at[0, 2], x_r.at[0, 2])
-    for d in NEAR:
-        to_z(d, 2, v_s, v_r)
-    await_z(3, 5)
-    await_z(4)
-
-    def products(*ds):
-        for d in ds:
-            for e in (1, 3) if d in NEAR else (1, 3) if d == 0 else (1, 3, 2):
-                await_block(d, e, x_s.at[d, e], x_r.at[d, e])
-            if d in NEAR:
-                await_block(d, 2, v_s.at[d], v_r.at[d])
-            for l in range(NY):
-                mloads[d, l].wait()
-        total = None
-        for d in ds:
-            base = zpos(NZ - d) * NX
-            for l in range(NY):
-                cols = []
-                for h in range(2):
-                    even = xg[base + 2 * h, 16 * l : 16 * l + 16, :]
-                    odd = xg[base + 2 * h + 1, 16 * l : 16 * l + 16, :]
-                    cols.append(jnp.concatenate(halves(even, odd), axis=0))
-                r = three(jnp.concatenate(cols, axis=1), mbuf[d, l], NT)
-                total = r if total is None else total + r
-        return total
-
-    coarse = products(0, 1, 7)
-    coarse += products(2, 6)
-
-    for i in (2, 3, 1):
-        remote(*odesc[i]).wait_recv()
+    for zp in range(1, NZ):
+        @pl.when(zp > z)
+        def _():
+            pl.semaphore_wait(z_in.at[zp], 1)
+            z_copy(zp).start()
+    inputs[2].wait()
+
+    @pl.when((cross_next & (z < NZ - 1)) | (cross_prev & (z == 0)))
+    def _():
+        pl.semaphore_wait(s_in, 1)
+
+    wdesc = [
+        (want_ref, nwant.at[0], w_s.at[0], w_r.at[0], (nxt, b)),
+        (want_ref, nwant.at[1], w_s.at[1], w_r.at[1], (prv, b)),
+    ]
     for args in wdesc:
-        remote(*args).wait_recv()
+        send(*args)
     hdesc = [
         (hout.at[0], hin.at[1], h_s.at[0], h_r.at[1], (prv, b)),
         (hout.at[1], hin.at[0], h_s.at[1], h_r.at[0], (nxt, b)),
     ]
-    for side in range(2):
+
+    for zp in EARLY:
+        forward(zp)
+    arrival(z, 2, o_r.at[z])
+    for d in NEAR:
+        v_copy(d).start()
+
+    def margin(side):
+        remote(*wdesc[side]).wait_recv()
         wanted = nwant[side, 0, 1 - side : 2 - side, :]
         total = None
         for i in range(NB):
@@ -245,10 +263,50 @@
             r = exact(res_ref[...] if i == 0 else own[i - 1], (rows == wanted).astype(BF16))
             total = r if total is None else total + r
         hout[side] = total
-    for args in hdesc:
-        send(*args)
-
-    coarse += products(3, 5, 4)
+        remote(*hdesc[side]).start()
+
+    late_prev = cross_prev & (z == 0)
+    for i in (2, 3, 1):
+        remote(*odesc[i]).wait_recv()
+    margin(1)
+
+    @pl.when(jnp.logical_not(late_prev))
+    def _():
+        margin(0)
+
+    def products(*zps):
+        for zp in zps:
+            for e in (1, 3):
+                arrival(zp, e, x_r.at[zp, e])
+
+            @pl.when(zp != z)
+            def _():
+                arrival(zp, 2, o_r.at[zp])
+
+            for l in range(NY):
+                mloads[zp, l].wait()
+        total = None
+        for zp in zps:
+            for l in range(NY):
+                cols = []
+                for h in range(2):
+                    even = xg[zp * NX + 2 * h, 16 * l : 16 * l + 16, :]
+                    odd = xg[zp * NX + 2 * h + 1, 16 * l : 16 * l + 16, :]
+                    cols.append(jnp.concatenate(halves(even, odd), axis=0))
+                r = three(jnp.concatenate(cols, axis=1), mbuf[zp, l], NT)
+                total = r if total is None else total + r
+        return total
+
+    for zp in LATE:
+        forward(zp)
+
+    @pl.when(late_prev)
+    def _():
+        margin(0)
+
+    coarse = products(*EARLY)
+    coarse += products(*LATE[:2])
+    coarse += products(*LATE[2:])
     ysum[0] = coarse
     adesc = {}
     for i in (2, 3, 1):
@@ -273,8 +331,21 @@
         remote(*adesc[i]).wait_recv()
     coarse = (ysum[0] + ysum[1]) + (ysum[2] + ysum[3])
     out_ref[...] = fine + exact(coarse, onehot)
-    for c in sent:
+    for c in sent + [remote(*args) for args in hdesc]:
         c.wait_send()
+    for zp in range(NZ):
+        @pl.when(zp != z)
+        def _():
+            z_copy(zp).wait_send()
+
+        @pl.when(jnp.logical_not(near(zp)))
+        def _():
+            x_copy(zp, 2).wait_send()
+
+        x_copy(zp, 1).wait_send()
+        x_copy(zp, 3).wait_send()
+    for d in NEAR:
+        v_copy(d).wait_send()
 
 
 def on_device(residual, fine_inverse, coarse_inverse, wanted_rows, wanted_count, aggregate):
@@ -311,7 +382,7 @@
             dma((2,)), dma((2,)),
             dma((2,)), dma((2,)),
             dma((NB,)), dma((NB,)),
-            pltpu.SemaphoreType.REGULAR,
+            pltpu.SemaphoreType.REGULAR((NZ,)), pltpu.SemaphoreType.REGULAR,
         ],
         compiler_params=pltpu.CompilerParams(
             collective_id=0, has_side_effects=True, vmem_limit_bytes=48 * 1024 * 1024

time: 31 us -> 29.3 us (0.945)
  Pallas kernels: 30.3 us -> 28.6 us
    pallas_call x1, Pallas kernels: 30.3 us -> 28.6 us  [on_device(): pl.pallas_call(kernel, out_shape=jax.ShapeDtypeStruct((PR, BL), F32), in_...]
where the time goes in v3:
time: 29.3 us; the launch traced here: 29.2 us
  Pallas kernels  28.6 us (98%)
  local copies, waits for them, and re-layouts  0.63 us (2%)
    pallas_call x1, Pallas kernels, on_device(): pl.pallas_call(kernel, out_shape=jax.ShapeDtypeStruct((PR, BL), F32), in_...  28.6 us
    unnamed x1, local copies, waits for them, and re-layouts  0.63 us

profile of v3, /device:TPU:1, one launch (start us, length us, event | category | flops | bytes accessed | tf_op | source)
XLA Modules:
  0.0 29.2 jit_solution(2258269109923971692)
XLA Ops:
  0.0 28.6 %schwarz.1 = f32[32,512]{1,0:T(8,128)S(1)} custom-call(f32[32,512]{1,0:T(8,128)} %res_hbm.1, s32[1,512]{1,0:T(1,128)} %bitcast.1, s32[1,2,256]{2,1,0:T(2,128)} %want_hbm.1, s32[1,2]{1,0:T(1,128)} %count_hbm.1, f32[256,1,4096]{2,1,0:T(1,128)} %m_hbm.1, f32[1,2560,512]{2,1,0:T(8,128)} %f_hbm.1), custom_call_target="tpu_custom_call" | custom-call | tf_op jit(solution)/shard_map/schwarz/pallas_call | solution.py:355
  28.6 0.6 %copy.8 = f32[32,512]{1,0:T(8,128)} copy(f32[32,512]{1,0:T(8,128)S(1)} %schwarz.1) | data formatting | bytes 131072

commit v4 on v3

--- a/solution.py
+++ b/solution.py
@@ -14,7 +14,8 @@
 HM = 256
 F32, BF16 = jnp.float32, jnp.bfloat16
 MESH = pl.DeviceIdType.MESH
-EARLY, LATE = (0, 1, 2, 3), (7, 6, 5, 4)
+EARLY, LATE = (0, 1, 2, 3), (7, 6, 4, 5)
+GROUPS = ((0, 1, 2, 3), (4, 5), (6, 7))
 NEAR = (1, 2, 7, 6)
 NN = (((1,), (0,)), ((), ()))
 NT = (((1,), (1,)), ((), ()))
@@ -53,7 +54,7 @@
 def kernel(
     res_hbm, agg_hbm, want_hbm, count_hbm, m_hbm, f_hbm, out_ref,
     res_ref, agg_ref, want_ref, count_ref, mbuf, fown, fmar, own, qout, ybuf, xg, nwant, hout, hin, ysum,
-    i_sem, m_sem, f_sem, g_sem, own_s, own_r, y_s, y_r, z_s, z_r, v_s, o_r, x_s, x_r, w_s, w_r, h_s, h_r, a_s, a_r, z_in, s_in,
+    i_sem, m_sem, f_sem, y_r, own_r, z_r, o_r, x_r, w_r, h_r, a_r, y_s, b_s, own_s, w_s, h_s, a_s, z_in, s_in,
 ):
     s = lax.axis_index("sub")
     b = lax.axis_index("blk")
@@ -133,22 +134,22 @@
             src_ref=src, dst_ref=dst, send_sem=ss, recv_sem=rs, device_id=to, device_id_type=MESH
         )
 
-    sent = []
-
     def send(*args):
-        c = remote(*args)
-        c.start()
-        sent.append(c)
-
-    ydesc = []
+        remote(*args).start()
+
+    def arrived(ref, sem):
+        remote(ref, ref, b_s, sem, (s, at_b[1])).wait_recv()
+
+    def departed(ref, sem):
+        remote(ref, ref, sem, y_r, (s, at_b[1])).wait_send()
+
     for other, i in ((0, 2), (0, 3), (1, 0), (1, 1), (1, 2), (1, 3), (0, 1)):
         to = at_b[i]
-        ydesc.append((qout.at[to], ybuf.at[other, i], y_s.at[other, i], y_r.at[other, i], (mate if other else s, to)))
-        send(*ydesc[-1])
+        send(qout.at[to], ybuf.at[i + NB * other - 1], y_s, y_r, (mate if other else s, to))
     for zp in range(NZ - 1):
         @pl.when(zp < z)
         def _():
-            signal(z_in.at[z], along_z(zp))
+            signal(z_in, along_z(zp))
 
     @pl.when(answers_prev)
     def _():
@@ -158,32 +159,34 @@
     def _():
         signal(s_in, (nxt, b))
 
-    loads = []
     for i in range(NB):
         rows = pl.ds(pl.multiple_of(HM + at_b[i] * BL, 256), BL)
-        loads.append(pltpu.make_async_copy(f_hbm.at[0, rows, :], fown.at[i], f_sem.at[i]))
+        pltpu.make_async_copy(f_hbm.at[0, rows, :], fown.at[i], f_sem.at[min(i, 1)]).start()
     for side in range(2):
         rows = pl.ds(side * (HM + NB * BL), HM)
-        loads.append(pltpu.make_async_copy(f_hbm.at[0, rows, :], fmar.at[side], g_sem.at[side]))
-    for c in loads:
-        c.start()
-    mloads = {}
-    for zp in range(NZ):
-        for l in range(NY):
-            cols = pl.ds(l * (NZ * CS) + zp * CS, CS)
-            mloads[zp, l] = pltpu.make_async_copy(m_hbm.at[:, 0, cols], mbuf.at[zp, l], m_sem.at[zp, l])
-            mloads[zp, l].start()
-    loads[0].wait()
+        pltpu.make_async_copy(f_hbm.at[0, rows, :], fmar.at[side], f_sem.at[2]).start()
+    for g, group in enumerate(GROUPS):
+        for zp in group:
+            for l in range(NY):
+                cols = pl.ds(l * (NZ * CS) + zp * CS, CS)
+                pltpu.make_async_copy(m_hbm.at[:, 0, cols], mbuf.at[zp, l], m_sem.at[g]).start()
+
+    def loaded(ref, sem):
+        pltpu.make_async_copy(ref, ref, sem).wait()
+
+    loaded(fown.at[0], f_sem.at[0])
     fine = three(res_ref[...], fown[0])
 
-    for args in ydesc:
-        remote(*args).wait_recv()
-    mine = (qout[b] + ybuf[0, 1]) + (ybuf[0, 2] + ybuf[0, 3])
-    theirs = (ybuf[1, 0] + ybuf[1, 1]) + (ybuf[1, 2] + ybuf[1, 3])
+    arrived(ybuf, y_r)
+    mine = (qout[b] + ybuf[0]) + (ybuf[1] + ybuf[2])
+    theirs = (ybuf[3] + ybuf[4]) + (ybuf[5] + ybuf[6])
     slot = z * NX + x
     xg[slot, pl.ds(pl.multiple_of(yl * 16, 16), 16), :] = mine
     xg[slot, pl.ds(pl.multiple_of((1 - yl) * 16, 16), 16), :] = theirs
 
+    def group_of(zp):
+        return jnp.where(zp >= 6, 2, jnp.where(zp >= 4, 1, 0)) if not isinstance(zp, int) else max(0, zp // 2 - 1)
+
     def block(zp, e):
         return xg.at[zp * NX + lax.rem(x + NX - e, NX)]
 
@@ -192,22 +195,18 @@
         return (d == 1) | (d == 2) | (d == 6) | (d == 7)
 
     def z_copy(zp):
-        return remote(block(z, 0), block(z, 0), z_s.at[zp], z_r.at[z], along_z(zp))
+        return remote(block(z, 0), block(z, 0), b_s, z_r.at[z], along_z(zp))
 
     def v_copy(d):
-        return remote(block(z, 2), block(z, 2), v_s.at[d], o_r.at[z], (at_z(d), b))
+        return remote(block(z, 2), block(z, 2), b_s, x_r.at[group_of(z)], (at_z(d), b))
 
     def x_copy(zp, e):
-        rs = o_r.at[zp] if e == 2 else x_r.at[zp, e]
-        return remote(block(zp, 0), block(zp, 0), x_s.at[zp, e], rs, (at_x(e), b))
-
-    def arrival(zp, e, rs):
-        remote(block(zp, e), block(zp, e), x_s.at[0, 0], rs, (s, at_b[1])).wait_recv()
+        return remote(block(zp, 0), block(zp, 0), b_s, x_r.at[group_of(zp)], (at_x(e), b))
 
     def forward(zp):
         @pl.when(zp != z)
         def _():
-            arrival(zp, 0, z_r.at[zp])
+            arrived(block(zp, 0), z_r.at[zp])
 
             @pl.when(jnp.logical_not(near(zp)))
             def _():
@@ -220,16 +219,19 @@
         @pl.when(zp < z)
         def _():
             z_copy(zp).start()
-    for e in (2, 1, 3):
+    send(block(z, 0), block(z, 0), b_s, o_r, (at_x(2), b))
+    for e in (1, 3):
         x_copy(z, e).start()
-    odesc = {}
     for i in (2, 3, 1):
-        odesc[i] = (res_ref, own.at[i - 1], own_s.at[i], own_r.at[i], (s, at_b[i]))
-        send(*odesc[i])
+        send(res_ref, own.at[i - 1], own_s, own_r, (s, at_b[i]))
+
+    @pl.when(z < NZ - 1)
+    def _():
+        pl.semaphore_wait(z_in, NZ - 1 - z)
+
     for zp in range(1, NZ):
         @pl.when(zp > z)
         def _():
-            pl.semaphore_wait(z_in.at[zp], 1)
             z_copy(zp).start()
     inputs[2].wait()
 
@@ -237,25 +239,17 @@
     def _():
         pl.semaphore_wait(s_in, 1)
 
-    wdesc = [
-        (want_ref, nwant.at[0], w_s.at[0], w_r.at[0], (nxt, b)),
-        (want_ref, nwant.at[1], w_s.at[1], w_r.at[1], (prv, b)),
-    ]
-    for args in wdesc:
-        send(*args)
-    hdesc = [
-        (hout.at[0], hin.at[1], h_s.at[0], h_r.at[1], (prv, b)),
-        (hout.at[1], hin.at[0], h_s.at[1], h_r.at[0], (nxt, b)),
-    ]
+    send(want_ref, nwant.at[0], w_s, w_r.at[0], (nxt, b))
+    send(want_ref, nwant.at[1], w_s, w_r.at[1], (prv, b))
 
     for zp in EARLY:
         forward(zp)
-    arrival(z, 2, o_r.at[z])
+    arrived(block(z, 2), o_r)
     for d in NEAR:
         v_copy(d).start()
 
     def margin(side):
-        remote(*wdesc[side]).wait_recv()
+        arrived(nwant.at[side], w_r.at[side])
         wanted = nwant[side, 0, 1 - side : 2 - side, :]
         total = None
         for i in range(NB):
@@ -263,28 +257,30 @@
             r = exact(res_ref[...] if i == 0 else own[i - 1], (rows == wanted).astype(BF16))
             total = r if total is None else total + r
         hout[side] = total
-        remote(*hdesc[side]).start()
+        send(hout.at[side], hin.at[1 - side], h_s, h_r, (nxt if side else prv, b))
 
     late_prev = cross_prev & (z == 0)
-    for i in (2, 3, 1):
-        remote(*odesc[i]).wait_recv()
+    arrived(own, own_r)
     margin(1)
 
     @pl.when(jnp.logical_not(late_prev))
     def _():
         margin(0)
 
-    def products(*zps):
-        for zp in zps:
-            for e in (1, 3):
-                arrival(zp, e, x_r.at[zp, e])
-
-            @pl.when(zp != z)
-            def _():
-                arrival(zp, 2, o_r.at[zp])
-
-            for l in range(NY):
-                mloads[zp, l].wait()
+    def products(g):
+        zps = GROUPS[g]
+        first, n = zps[0] * NX, NX * len(zps) - len(zps)
+        has_own = (z >= zps[0]) & (z <= zps[-1])
+
+        @pl.when(has_own)
+        def _():
+            arrived(xg.at[pl.ds(first, n - 1)], x_r.at[g])
+
+        @pl.when(jnp.logical_not(has_own))
+        def _():
+            arrived(xg.at[pl.ds(first, n)], x_r.at[g])
+
+        loaded(mbuf.at[pl.ds(zps[0], len(zps))], m_sem.at[g])
         total = None
         for zp in zps:
             for l in range(NY):
@@ -304,48 +300,34 @@
     def _():
         margin(0)
 
-    coarse = products(*EARLY)
-    coarse += products(*LATE[:2])
-    coarse += products(*LATE[2:])
+    coarse = products(0)
+    coarse += products(2)
+    coarse += products(1)
     ysum[0] = coarse
-    adesc = {}
     for i in (2, 3, 1):
-        adesc[i] = (ysum.at[0], ysum.at[i], a_s.at[i], a_r.at[i], (s, at_b[i]))
-        send(*adesc[i])
-
-    for i in range(1, NB):
-        loads[i].wait()
+        send(ysum.at[0], ysum.at[i], a_s, a_r, (s, at_b[i]))
+
+    loaded(fown.at[pl.ds(1, NB - 1)], f_sem.at[1])
     for i in range(1, NB):
         fine += three(own[i - 1], fown[i])
     inputs[3].wait()
     slots = lax.broadcasted_iota(jnp.int32, (PR, HM), 1)
-    for side in range(2):
-        remote(*hdesc[1 - side]).wait_recv()
-        loads[NB + side].wait()
+    arrived(hin, h_r)
+    loaded(fmar, f_sem.at[2])
     for side in range(2):
         edge = s == (0 if side == 0 else NSUB - 1)
         kept = jnp.where(edge, 0, count_ref[0, side])
         fine += three(jnp.where(slots < kept, hin[side], 0.0), fmar[side])
 
-    for i in (1, 2, 3):
-        remote(*adesc[i]).wait_recv()
+    arrived(ysum.at[pl.ds(1, NB - 1)], a_r)
     coarse = (ysum[0] + ysum[1]) + (ysum[2] + ysum[3])
     out_ref[...] = fine + exact(coarse, onehot)
-    for c in sent + [remote(*args) for args in hdesc]:
-        c.wait_send()
-    for zp in range(NZ):
-        @pl.when(zp != z)
-        def _():
-            z_copy(zp).wait_send()
-
-        @pl.when(jnp.logical_not(near(zp)))
-        def _():
-            x_copy(zp, 2).wait_send()
-
-        x_copy(zp, 1).wait_send()
-        x_copy(zp, 3).wait_send()
-    for d in NEAR:
-        v_copy(d).wait_send()
+    departed(ybuf, y_s)
+    departed(xg.at[pl.ds(0, 31)], b_s)
+    departed(own, own_s)
+    departed(nwant, w_s)
+    departed(hout, h_s)
+    departed(ysum.at[pl.ds(1, NB - 1)], a_s)
 
 
 def on_device(residual, fine_inverse, coarse_inverse, wanted_rows, wanted_count, aggregate):
@@ -367,22 +349,16 @@
             pltpu.VMEM((2, HM, BL), F32),
             pltpu.VMEM((NB - 1, PR, BL), F32),
             pltpu.VMEM((NB, PR // 2, 128), F32),
-            pltpu.VMEM((2, NB, PR // 2, 128), F32),
+            pltpu.VMEM((2 * NB - 1, PR // 2, 128), F32),
             pltpu.VMEM((NZ * NX, PR, 128), F32),
             pltpu.VMEM((2, 1, 2, HM), jnp.int32),
             pltpu.VMEM((2, PR, HM), F32),
             pltpu.VMEM((2, PR, HM), F32),
             pltpu.VMEM((NB, PR, CS), F32),
-            dma((4,)), dma((NZ, NY)), dma((NB,)), dma((2,)),
-            dma((NB,)), dma((NB,)),
-            dma((2, NB)), dma((2, NB)),
-            dma((NZ,)), dma((NZ,)),
-            dma((NZ,)), dma((NZ,)),
-            dma((NZ, NX)), dma((NZ, NX)),
-            dma((2,)), dma((2,)),
-            dma((2,)), dma((2,)),
-            dma((NB,)), dma((NB,)),
-            pltpu.SemaphoreType.REGULAR((NZ,)), pltpu.SemaphoreType.REGULAR,
+            dma((4,)), dma((3,)), dma((3,)),
+            dma, dma, dma((NZ,)), dma, dma((3,)), dma((2,)), dma, dma,
+            dma, dma, dma, dma, dma, dma,
+            pltpu.SemaphoreType.REGULAR, pltpu.SemaphoreType.REGULAR,
         ],
         compiler_params=pltpu.CompilerParams(
             collective_id=0, has_side_effects=True, vmem_limit_bytes=48 * 1024 * 1024

time: 29.3 us -> 28.8 us (0.983)
  Pallas kernels: 28.6 us -> 28.1 us
    pallas_call x1, Pallas kernels: 28.6 us -> 28.1 us  [on_device(): pl.pallas_call(kernel, out_shape=jax.ShapeDtypeStruct((PR, BL), F32), in_...]
where the time goes in v4:
time: 28.8 us; the launch traced here: 28.7 us
  Pallas kernels  28.1 us (98%)
  local copies, waits for them, and re-layouts  0.63 us (2%)
    pallas_call x1, Pallas kernels, on_device(): pl.pallas_call(kernel, out_shape=jax.ShapeDtypeStruct((PR, BL), F32), in_...  28.1 us
    unnamed x1, local copies, waits for them, and re-layouts  0.63 us

profile of v4, /device:TPU:1, one launch (start us, length us, event | category | flops | bytes accessed | tf_op | source)
XLA Modules:
  0.0 28.7 jit_solution(15518186789992958049)
XLA Ops:
  0.0 28.1 %schwarz.1 = f32[32,512]{1,0:T(8,128)S(1)} custom-call(f32[32,512]{1,0:T(8,128)} %res_hbm.1, s32[1,512]{1,0:T(1,128)} %bitcast.1, s32[1,2,256]{2,1,0:T(2,128)} %want_hbm.1, s32[1,2]{1,0:T(1,128)} %count_hbm.1, f32[256,1,4096]{2,1,0:T(1,128)} %m_hbm.1, f32[1,2560,512]{2,1,0:T(8,128)} %f_hbm.1), custom_call_target="tpu_custom_call" | custom-call | tf_op jit(solution)/shard_map/schwarz/pallas_call | solution.py:337
  28.1 0.6 %copy.8 = f32[32,512]{1,0:T(8,128)} copy(f32[32,512]{1,0:T(8,128)S(1)} %schwarz.1) | data formatting | bytes 131072

commit v5 on v4

--- a/solution.py
+++ b/solution.py
@@ -16,7 +16,6 @@
 MESH = pl.DeviceIdType.MESH
 EARLY, LATE = (0, 1, 2, 3), (7, 6, 4, 5)
 GROUPS = ((0, 1, 2, 3), (4, 5), (6, 7))
-NEAR = (1, 2, 7, 6)
 NN = (((1,), (0,)), ((), ()))
 NT = (((1,), (1,)), ((), ()))
 
@@ -54,7 +53,7 @@
 def kernel(
     res_hbm, agg_hbm, want_hbm, count_hbm, m_hbm, f_hbm, out_ref,
     res_ref, agg_ref, want_ref, count_ref, mbuf, fown, fmar, own, qout, ybuf, xg, nwant, hout, hin, ysum,
-    i_sem, m_sem, f_sem, y_r, own_r, z_r, o_r, x_r, w_r, h_r, a_r, y_s, b_s, own_s, w_s, h_s, a_s, z_in, s_in,
+    i_sem, m_sem, f_sem, y_r, own_r, z_r, x_r, w_r, h_r, a_r, y_s, b_s, own_s, w_s, h_s, a_s, z_in, s_in,
 ):
     s = lax.axis_index("sub")
     b = lax.axis_index("blk")
@@ -62,12 +61,6 @@
     z = lax.rem(s // NX, NZ)
     x = lax.rem(s, NX)
     mate = lax.rem(s + NZ * NX, NSUB)
-
-    def zpos(d):
-        return lax.rem(z + d, NZ)
-
-    def at_z(d):
-        return yl * (NZ * NX) + zpos(d) * NX + x
 
     def at_x(d):
         return s - x + lax.rem(x + d, NX)
@@ -190,16 +183,9 @@
     def block(zp, e):
         return xg.at[zp * NX + lax.rem(x + NX - e, NX)]
 
-    def near(zp):
-        d = lax.rem(z + NZ - zp, NZ)
-        return (d == 1) | (d == 2) | (d == 6) | (d == 7)
-
     def z_copy(zp):
         return remote(block(z, 0), block(z, 0), b_s, z_r.at[z], along_z(zp))
 
-    def v_copy(d):
-        return remote(block(z, 2), block(z, 2), b_s, x_r.at[group_of(z)], (at_z(d), b))
-
     def x_copy(zp, e):
         return remote(block(zp, 0), block(zp, 0), b_s, x_r.at[group_of(zp)], (at_x(e), b))
 
@@ -208,19 +194,14 @@
         def _():
             arrived(block(zp, 0), z_r.at[zp])
 
-            @pl.when(jnp.logical_not(near(zp)))
-            def _():
-                x_copy(zp, 2).start()
-
-            x_copy(zp, 1).start()
-            x_copy(zp, 3).start()
+            for e in (2, 1, 3):
+                x_copy(zp, e).start()
 
     for zp in range(NZ - 1):
         @pl.when(zp < z)
         def _():
             z_copy(zp).start()
-    send(block(z, 0), block(z, 0), b_s, o_r, (at_x(2), b))
-    for e in (1, 3):
+    for e in (2, 1, 3):
         x_copy(z, e).start()
     for i in (2, 3, 1):
         send(res_ref, own.at[i - 1], own_s, own_r, (s, at_b[i]))
@@ -244,9 +225,6 @@
 
     for zp in EARLY:
         forward(zp)
-    arrived(block(z, 2), o_r)
-    for d in NEAR:
-        v_copy(d).start()
 
     def margin(side):
         arrived(nwant.at[side], w_r.at[side])
@@ -269,17 +247,7 @@
 
     def products(g):
         zps = GROUPS[g]
-        first, n = zps[0] * NX, NX * len(zps) - len(zps)
-        has_own = (z >= zps[0]) & (z <= zps[-1])
-
-        @pl.when(has_own)
-        def _():
-            arrived(xg.at[pl.ds(first, n - 1)], x_r.at[g])
-
-        @pl.when(jnp.logical_not(has_own))
-        def _():
-            arrived(xg.at[pl.ds(first, n)], x_r.at[g])
-
+        arrived(xg.at[pl.ds(zps[0] * NX, (NX - 1) * len(zps))], x_r.at[g])
         loaded(mbuf.at[pl.ds(zps[0], len(zps))], m_sem.at[g])
         total = None
         for zp in zps:
@@ -356,7 +324,7 @@
             pltpu.VMEM((2, PR, HM), F32),
             pltpu.VMEM((NB, PR, CS), F32),
             dma((4,)), dma((3,)), dma((3,)),
-            dma, dma, dma((NZ,)), dma, dma((3,)), dma((2,)), dma, dma,
+            dma, dma, dma((NZ,)), dma((3,)), dma((2,)), dma, dma,
             dma, dma, dma, dma, dma, dma,
             pltpu.SemaphoreType.REGULAR, pltpu.SemaphoreType.REGULAR,
         ],

time: 28.8 us -> 28 us (0.972)
  Pallas kernels: 28.1 us -> 27.3 us
    pallas_call x1, Pallas kernels: 28.1 us -> 27.3 us  [on_device(): pl.pallas_call(kernel, out_shape=jax.ShapeDtypeStruct((PR, BL), F32), in_...]
where the time goes in v5:
time: 28 us; the launch traced here: 27.9 us
  Pallas kernels  27.3 us (98%)
  local copies, waits for them, and re-layouts  0.63 us (2%)
    pallas_call x1, Pallas kernels, on_device(): pl.pallas_call(kernel, out_shape=jax.ShapeDtypeStruct((PR, BL), F32), in_...  27.3 us
    unnamed x1, local copies, waits for them, and re-layouts  0.63 us

profile of v5, /device:TPU:1, one launch (start us, length us, event | category | flops | bytes accessed | tf_op | source)
XLA Modules:
  0.0 27.9 jit_solution(8577635237122753969)
XLA Ops:
  0.0 27.3 %schwarz.1 = f32[32,512]{1,0:T(8,128)S(1)} custom-call(f32[32,512]{1,0:T(8,128)} %res_hbm.1, s32[1,512]{1,0:T(1,128)} %bitcast.1, s32[1,2,256]{2,1,0:T(2,128)} %want_hbm.1, s32[1,2]{1,0:T(1,128)} %count_hbm.1, f32[256,1,4096]{2,1,0:T(1,128)} %m_hbm.1, f32[1,2560,512]{2,1,0:T(8,128)} %f_hbm.1), custom_call_target="tpu_custom_call" | custom-call | tf_op jit(solution)/shard_map/schwarz/pallas_call | solution.py:305
  27.3 0.6 %copy.8 = f32[32,512]{1,0:T(8,128)} copy(f32[32,512]{1,0:T(8,128)S(1)} %schwarz.1) | data formatting | bytes 131072

commit v6 on v5

--- a/solution.py
+++ b/solution.py
@@ -236,14 +236,6 @@
             total = r if total is None else total + r
         hout[side] = total
         send(hout.at[side], hin.at[1 - side], h_s, h_r, (nxt if side else prv, b))
-
-    late_prev = cross_prev & (z == 0)
-    arrived(own, own_r)
-    margin(1)
-
-    @pl.when(jnp.logical_not(late_prev))
-    def _():
-        margin(0)
 
     def products(g):
         zps = GROUPS[g]
@@ -264,10 +256,9 @@
     for zp in LATE:
         forward(zp)
 
-    @pl.when(late_prev)
-    def _():
-        margin(0)
-
+    arrived(own, own_r)
+    margin(1)
+    margin(0)
     coarse = products(0)
     coarse += products(2)
     coarse += products(1)

time: 28 us -> 28 us (level)
  no operation moved by 1% of the time
where the time goes in v6:
time: 28 us; the launch traced here: 27.8 us
  Pallas kernels  27.2 us (97%)
  local copies, waits for them, and re-layouts  0.63 us (2%)
    pallas_call x1, Pallas kernels, on_device(): pl.pallas_call(kernel, out_shape=jax.ShapeDtypeStruct((PR, BL), F32), in_...  27.2 us
    unnamed x1, local copies, waits for them, and re-layouts  0.63 us

profile of v6, /device:TPU:1, one launch (start us, length us, event | category | flops | bytes accessed | tf_op | source)
XLA Modules:
  0.0 27.8 jit_solution(14263401316610089178)
XLA Ops:
  0.0 27.2 %schwarz.1 = f32[32,512]{1,0:T(8,128)S(1)} custom-call(f32[32,512]{1,0:T(8,128)} %res_hbm.1, s32[1,512]{1,0:T(1,128)} %bitcast.1, s32[1,2,256]{2,1,0:T(2,128)} %want_hbm.1, s32[1,2]{1,0:T(1,128)} %count_hbm.1, f32[256,1,4096]{2,1,0:T(1,128)} %m_hbm.1, f32[1,2560,512]{2,1,0:T(8,128)} %f_hbm.1), custom_call_target="tpu_custom_call" | custom-call | tf_op jit(solution)/shard_map/schwarz/pallas_call | solution.py:296
  27.2 0.6 %copy.8 = f32[32,512]{1,0:T(8,128)} copy(f32[32,512]{1,0:T(8,128)S(1)} %schwarz.1) | data formatting | bytes 131072
